TPU v7x, 32 devices: a whole 2x2x4 slice. The times are simulated.
32 devices in a mesh: dp: 4 (over y, core), expert: 8 (over z, x).
Axes of the slice: x: 2, y: 2, z: 4, core: 2. Of those that a mesh axis runs over, the one named last changes fastest.
Arguments:
- hidden_in: bfloat16 [2048, 2048], P(('dp', 'expert')), may hold values from -6 to 6
- context: bfloat16 [2048, 2048], P(('dp', 'expert')), may hold values from -6 to 6
- out_proj: bfloat16 [2048, 2048], P(('dp', 'expert')), may hold values from -0.125 to 0.125
- norm_gain: float32 [2048], replicated, may hold values from 0.5 to 1.5
- router: bfloat16 [2048, 64], P(('dp', 'expert')), may hold values from -0.25 to 0.25
- expert_ids: int32 [2048, 8], P(('dp', 'expert')), may hold values from 0 to 63, as said below
- replica_expert: int32 [128], replicated, may hold values from 0 to 63, as said below
- split_pick: int32 [2048, 8], P(('dp', 'expert')), may hold values from 0 to 65535
- up_gate: bfloat16 [128, 2048, 2048], P(('dp', 'expert')), may hold values from -0.125 to 0.125
- down: bfloat16 [128, 1024, 2048], P(('dp', 'expert')), may hold values from -0.1875 to 0.1875
Outputs:
- layer_out: bfloat16 [2048, 2048], P(('dp', 'expert'))
Inputs may be any that keep to these rules, and one draw needn't show every extreme that they name: `expert_ids`: each row names 8 different experts. `replica_expert`: every expert is served by one replica or more.
All inputs are finite; a program needn't handle non-finite values.
Results may differ from a plain program's by a relative error of at most 0.004.
Values may be sent and summed in bfloat16 or wider, within the bound.
A program may use at most 128 MiB of HBM per device.

v0:
```python
import jax
import jax.numpy as jnp
from jax import lax
from jax.sharding import PartitionSpec as P


def rms_norm(residual, norm_gain):
    scale_back = lax.rsqrt(jnp.mean(residual * residual, axis=-1, keepdims=True) + 1e-05)
    return (residual * scale_back * norm_gain).astype(jnp.bfloat16)


def route_block(expert_ids, split_pick, replica_expert):
    replica_total = replica_expert.shape[0]
    replica_iota = lax.iota(jnp.int32, replica_total)
    same_expert = replica_expert[:, None] == replica_expert[None, :]
    earlier = replica_iota[:, None] > replica_iota[None, :]
    replica_rank = jnp.sum((same_expert & earlier).astype(jnp.int32), axis=1)
    serves = expert_ids[:, :, None] == replica_expert[None, None, :]
    replica_count = jnp.sum(serves.astype(jnp.int32), axis=-1)
    wanted = split_pick % replica_count
    matches = serves & (replica_rank[None, None, :] == wanted[:, :, None])
    replica = jnp.sum(jnp.where(matches, replica_iota[None, None, :], 0), axis=-1)
    flat_replica = replica.reshape(-1)
    pair_iota = lax.iota(jnp.int32, flat_replica.shape[0])
    same_target = flat_replica[:, None] == flat_replica[None, :]
    before = pair_iota[:, None] > pair_iota[None, :]
    slot_index = jnp.sum((same_target & before).astype(jnp.int32), axis=1)
    return (replica, slot_index.reshape(replica.shape))


def apply_experts(incoming, up_gate, down, capacity):
    arrived_shape = incoming.shape
    local_reps = up_gate.shape[0]
    hidden_units = down.shape[1]
    stacked = incoming.reshape(-1, local_reps, capacity, incoming.shape[-1])
    gate_up = jnp.einsum("sjcd,jdf->sjcf", stacked, up_gate, preferred_element_type=jnp.float32)
    hidden_act = (jax.nn.silu(gate_up[..., :hidden_units]) * gate_up[..., hidden_units:]).astype(
        jnp.bfloat16
    )
    expert_out = jnp.einsum("sjcf,jfd->sjcd", hidden_act, down, preferred_element_type=jnp.float32)
    return expert_out.astype(jnp.bfloat16).reshape(arrived_shape)


def per_device(
    hidden_in,
    context,
    out_proj,
    norm_gain,
    router,
    expert_ids,
    replica_expert,
    split_pick,
    up_gate,
    down,
):
    tok_rows, model_width = hidden_in.shape
    top_count = expert_ids.shape[1]
    replica_total = replica_expert.shape[0]
    local_reps = up_gate.shape[0]
    data_groups = lax.axis_size("dp")
    expert_groups = lax.axis_size("expert")
    capacity = max(2, 2 * tok_rows * top_count // replica_total)
    summed = jnp.dot(
        context,
        lax.all_gather(out_proj, ("dp", "expert"), axis=0, tiled=True),
        preferred_element_type=jnp.float32,
    )
    router_rows = lax.all_gather(router, ("dp", "expert"), axis=0, tiled=True)
    residual = hidden_in.astype(jnp.float32) + summed
    normed = rms_norm(residual, norm_gain)
    logits = jnp.dot(normed, router_rows, preferred_element_type=jnp.float32)
    hit_mask = expert_ids[:, :, None] == lax.iota(jnp.int32, logits.shape[1])[None, None, :]
    chosen = jnp.sum(jnp.where(hit_mask, logits[:, None, :], 0.0), axis=-1)
    raised = jnp.exp(chosen)
    route_weight = raised / jnp.sum(raised, axis=-1, keepdims=True)
    replica, slot_index = route_block(expert_ids, split_pick, replica_expert)
    within_cap = slot_index < capacity
    buffer_row = jnp.where(within_cap, replica * capacity + slot_index, -1).reshape(-1)
    slot_total = replica_total * capacity
    matches = buffer_row[None, :] == lax.iota(jnp.int32, slot_total)[:, None]
    filled = jnp.any(matches, axis=1)
    row_of_pair = lax.iota(jnp.int32, tok_rows * top_count) // top_count
    anchor = jnp.sum(jnp.where(matches, row_of_pair[None, :], 0), axis=1)
    outgoing = jnp.where(filled[:, None], normed[anchor], jnp.zeros((), jnp.bfloat16))
    outgoing = outgoing.reshape(data_groups, expert_groups, local_reps * capacity, model_width)
    incoming = lax.all_to_all(
        lax.all_to_all(outgoing, "expert", split_axis=1, concat_axis=1, tiled=True),
        "dp",
        split_axis=0,
        concat_axis=0,
        tiled=True,
    )
    results = apply_experts(incoming, up_gate, down, capacity)
    returned = lax.all_to_all(
        lax.all_to_all(results, "dp", split_axis=0, concat_axis=0, tiled=True),
        "expert",
        split_axis=1,
        concat_axis=1,
        tiled=True,
    )
    returned = returned.reshape(slot_total, model_width)
    safe_index = jnp.where(within_cap, replica * capacity + slot_index, 0)
    gathered = returned[safe_index]
    kept_weight = jnp.where(within_cap, route_weight, 0.0)
    layer_out = residual + jnp.sum(kept_weight[:, :, None] * gathered.astype(jnp.float32), axis=1)
    return layer_out.astype(jnp.bfloat16)


def solution(mesh):
    return jax.shard_map(
        per_device,
        mesh=mesh,
        in_specs=(
            P(("dp", "expert"), None),
            P(("dp", "expert"), None),
            P(("dp", "expert"), None),
            P(),
            P(("dp", "expert"), None),
            P(("dp", "expert"), None),
            P(),
            P(("dp", "expert"), None),
            P(("dp", "expert"), None, None),
            P(("dp", "expert"), None, None),
        ),
        out_specs=P(("dp", "expert"), None),
        check_vma=False,
    )
```

profile of v0, /device:TPU:0, one launch (start us, length us, event | category | flops | bytes accessed | tf_op | source)
XLA Modules:
  0.0 520.4 jit_solution(7582275169445691453)
XLA Ops:
  6.5 0.0 copy-start
  6.5 0.0 all-gather.2.cloned.1.call-start
  6.5 0.7 all-gather.2.cloned.1.call-update
  7.3 0.8 copy.38
  8.0 0.8 copy.39
  8.8 0.9 convert_reduce_fusion.1
  9.7 1.9 fusion.16
  11.6 0.4 add_select_fusion
  12.0 2.0 select_reduce_fusion.2
  13.9 0.1 eq.94
  14.0 0.3 convert_reduce_fusion
  14.3 0.3 fusion.14
  14.6 0.1 broadcast_in_dim.93
  14.7 0.3 select_reduce_fusion
  15.0 0.0 copy-start.3
  15.0 75.5 %all-gather.2.cloned.1.call-done = bf16[2048,2048]{1,0:T(8,128)(2,1)} async-done(((bf16[64,2048]{1,0:T(8,128)(2,1)}), bf16[2048,2048]{1,0:T(8,128)(2,1)}) %all-gather.2.cloned.1.call-update) | async-done | bytes 8388624 | tf_op jit(solution)/shard_map/all_gather | solution.py:65
  90.5 0.0 copy-done
  90.5 5.1 multiply_reduce_fusion
  95.6 0.0 copy-done.3
  95.6 0.1 multiply_convert_fusion
  95.7 6.0 %gather_fusion = bf16[1024,2048]{1,0:T(8,128)(2,1)} fusion(bf16[64,2048]{1,0:T(8,128)(2,1)S(1)} %multiply_convert_fusion, s32[1024]{0:T(1024)S(1)} %broadcast_clamp_fusion), kind=kCustom, calls=%fused_computation | custom fusion | bytes 8392704 | tf_op jit(solution)/shard_map/gather | solution.py:84
  101.7 2.5 copy_select_fusion
  104.2 97.4 %all_to_all.20 = bf16[4,8,32,2048]{3,2,0,1:T(8,128)(2,1)S(1)} all-to-all(bf16[4,8,32,2048]{3,2,0,1:T(8,128)(2,1)S(1)} %copy_select_fusion), channel_id=1, replica_groups=mesh['dp'=4,'expert'=8] {'expert'}, dimensions={1} | all-to-all | bytes 8388608 | tf_op jit(solution)/shard_map/all_to_all | solution.py:87
  201.6 0.6 copy.43
  202.2 51.7 %all_to_all.21 = bf16[4,8,32,2048]{3,2,1,0:T(8,128)(2,1)} all-to-all(bf16[4,8,32,2048]{3,2,1,0:T(8,128)(2,1)S(1)} %copy.43), channel_id=1, replica_groups=mesh['dp'=4,'expert'=8] {'dp'}, dimensions={0} | all-to-all | bytes 8388608 | tf_op jit(solution)/shard_map/all_to_all | solution.py:86
  253.9 18.3 %fusion.4 = f32[32,4,8,2048]{3,2,0,1:T(8,128)} fusion(bf16[4,2048,2048]{2,1,0:T(8,128)(2,1)} %param.18, bf16[32,4,8,2048]{3,2,1,0:T(8,128)(2,1)} %bitcast.39), kind=kOutput, calls=%fused_computation.6 | convolution fusion | flops 8589934592 | bytes 46137344 | tf_op jit(solution)/shard_map/sjcd,jdf->sjcf/dot_general | solution.py:36
  272.1 14.8 %convert_bitcast_fusion = bf16[32,4,8,2048]{3,2,0,1:T(8,128)(2,1)} fusion(bf16[4,1024,2048]{2,1,0:T(8,128)(2,1)} %param.19, f32[32,4,8,2048]{3,2,0,1:T(8,128)} %fusion.4), kind=kOutput, calls=%fused_computation.13 | convolution fusion | flops 4303355904 | bytes 29360128 | tf_op jit(solution)/shard_map/sjcf,jfd->sjcd/dot_general | solution.py:40
  287.0 2.5 copy.45
  289.5 50.7 %all_to_all.22 = bf16[4,8,32,2048]{3,2,1,0:T(8,128)(2,1)S(1)} all-to-all(bf16[4,8,32,2048]{3,2,1,0:T(8,128)(2,1)S(1)} %bitcast.42), channel_id=1, replica_groups=mesh['dp'=4,'expert'=8] {'dp'}, dimensions={0} | all-to-all | bytes 8388608 | tf_op jit(solution)/shard_map/all_to_all | solution.py:95
  340.2 2.3 copy.46
  342.5 0.0 copy-start.2
  342.5 4.7 all-to-all-start.3
  347.2 0.1 reshape.142
  347.3 0.1 lt.57
  347.4 0.1 reshape.153
  347.5 0.0 copy-done.2
  347.5 150.8 %all_gather.7 = bf16[2048,64]{1,0:T(8,128)(2,1)S(1)} all-gather(bf16[64,64]{1,0:T(8,128)(2,1)S(1)} %copy-done.2), channel_id=1, replica_groups=mesh['dp'=4,'expert'=8] {'dp','expert'}, dimensions={0}, use_global_device_ids=true | all-gather | bytes 270336 | tf_op jit(solution)/shard_map/all_gather | solution.py:68
  498.3 0.2 fusion.23
  498.6 0.2 select_reduce_fusion.1
  498.8 0.1 exponential_reduce_fusion
  498.9 0.1 divide_select_fusion
  499.0 0.0 all-to-all-done.3
  499.0 4.7 copy.47
  503.8 0.0 copy-start.1
  503.8 7.2 %gather_fusion.1 = bf16[512,2048]{1,0:T(8,128)(2,1)S(1)} fusion(bf16[1024,2048]{1,0:T(8,128)(2,1)} %bitcast.40, s32[1024]{0:T(1024)S(1)} %pad_clamp_fusion), kind=kCustom, calls=%fused_computation.1 | custom fusion | bytes 4196352 | tf_op jit(solution)/shard_map/gather | solution.py:103
  511.0 1.8 fusion.8
  512.8 0.8 add_convert_fusion
  513.6 0.0 copy-done.1
  (8 shorter events, 0.1 us)
Async XLA Ops:
  6.5 84.0 %copy-start = (bf16[64,2048]{1,0:T(8,128)(2,1)S(1)}, bf16[64,2048]{1,0:T(8,128)(2,1)}, u32[]{:S(2)}) copy-start(bf16[64,2048]{1,0:T(8,128)(2,1)} %param.11) | copy-start | bytes 786436
  6.5 84.0 %all-gather.2.cloned.1.call-start = ((), (), s32[]{:S(2)}) async-start(), calls=%async_computation.4 | async-start | bytes 8650752 | tf_op jit(solution)/shard_map/all_gather | solution.py:65
  15.0 80.6 %copy-start.3 = (f32[2048]{0:T(1024)S(1)}, f32[2048]{0:T(1024)}, u32[]{:S(2)}) copy-start(f32[2048]{0:T(1024)} %param.13) | copy-start | bytes 24580
  342.5 5.0 copy-start.2
  342.5 156.5 %all-to-all-start.3 = ((bf16[4,8,32,2048]{3,2,0,1:T(8,128)(2,1)}), bf16[4,8,32,2048]{3,2,0,1:T(8,128)(2,1)}, u32[]{:S(2)}, u32[]{:S(2)}) async-start(bf16[4,8,32,2048]{3,2,0,1:T(8,128)(2,1)} %copy.46), calls=%async_computation.3 | async-start | bytes 8388608 | tf_op jit(solution)/shard_map/all_to_all | solution.py:94
  503.8 9.8 %copy-start.1 = (bf16[64,2048]{1,0:T(8,128)(2,1)S(1)}, bf16[64,2048]{1,0:T(8,128)(2,1)}, u32[]{:S(2)}) copy-start(bf16[64,2048]{1,0:T(8,128)(2,1)} %param.11) | copy-start | bytes 786436
Sparse Core Ops, SparseCore 0:
  10.3 80.1 all-gather.1
where the time goes:
time: 521 us; the launch traced here: 520 us
  blocking collectives  351 us (67%)
  waiting for transfers between devices  76.2 us (15%)
  matrix products  38.4 us (7%)
  local copies, waits for them, and re-layouts  25.3 us (5%)
  between operations  13.6 us (3%)
  other arithmetic  11.6 us (2%)
    all_gather x1, blocking collectives, per_device(): router_rows = lax.all_gather(router, ('dp', 'expert'), axis=0, tiled=True)  151 us
    all_to_all x1, blocking collectives, per_device(): lax.all_to_all(outgoing, 'expert', split_axis=1, concat_axis=1, tiled=True)  97.4 us
    all_gather x1, waiting for transfers between devices, per_device(): lax.all_gather(out_proj, ('dp', 'expert'), axis=0, tiled=True)  75.5 us
    all_to_all x1, blocking collectives, per_device(): lax.all_to_all(lax.all_to_all(outgoing, 'expert', split_axis=1, concat_ax...  51.7 us
    all_to_all x1, blocking collectives, per_device(): lax.all_to_all(results, 'dp', split_axis=0, concat_axis=0, tiled=True)  50.7 us
    dot_general x1, matrix products, apply_experts(): jnp.einsum('sjcd,jdf->sjcf', stacked, up_gate, preferred_element_type=jnp...  18.3 us
    dot_general x1, matrix products, apply_experts(): jnp.einsum('sjcf,jfd->sjcd', hidden_act, down, preferred_element_type=jnp...  14.8 us
  transfers between devices with their start and end apart: 2, of which 1 were waited for; matrix products, arithmetic and copies ran while one was open for 2% of the time, Pallas kernels for 0%

commit v1 on v0

--- a/solution.py
+++ b/solution.py
@@ -106,9 +106,76 @@
     return layer_out.astype(jnp.bfloat16)
 
 
+def per_device_gathered(
+    hidden_in,
+    context,
+    out_proj,
+    norm_gain,
+    router,
+    expert_ids,
+    replica_expert,
+    split_pick,
+    up_gate,
+    down,
+):
+    axes = ("dp", "expert")
+    tok_rows, model_width = hidden_in.shape
+    top_count = expert_ids.shape[1]
+    replica_total = replica_expert.shape[0]
+    local_reps = up_gate.shape[0]
+    hidden_units = down.shape[1]
+    blocks = lax.axis_size("dp") * lax.axis_size("expert")
+    me = lax.axis_index("dp") * lax.axis_size("expert") + lax.axis_index("expert")
+    capacity = max(2, 2 * tok_rows * top_count // replica_total)
+    local_slots = local_reps * capacity
+    proj_rows = lax.all_gather(out_proj, axes, axis=0, tiled=True)
+    router_rows = lax.all_gather(router, axes, axis=0, tiled=True)
+    replica, slot_index = route_block(expert_ids, split_pick, replica_expert)
+    position = jnp.where(slot_index < capacity, replica * capacity + slot_index, -1)
+    positions = lax.all_gather(position, axes, axis=0, tiled=False)
+    summed = jnp.dot(context, proj_rows, preferred_element_type=jnp.float32)
+    residual = hidden_in.astype(jnp.float32) + summed
+    normed = rms_norm(residual, norm_gain)
+    all_normed = lax.all_gather(normed, axes, axis=0, tiled=False)
+    logits = jnp.dot(normed, router_rows, preferred_element_type=jnp.float32)
+    hit_mask = expert_ids[:, :, None] == lax.iota(jnp.int32, logits.shape[1])[None, None, :]
+    chosen = jnp.sum(jnp.where(hit_mask, logits[:, None, :], 0.0), axis=-1)
+    raised = jnp.exp(chosen)
+    route_weight = raised / jnp.sum(raised, axis=-1, keepdims=True)
+    weights = lax.all_gather(route_weight, axes, axis=0, tiled=False)
+    local_iota = lax.iota(jnp.int32, local_slots)
+    hits = (positions - me * local_slots)[:, :, :, None] == local_iota
+    pick = jnp.any(hits, axis=2)
+    slot_weight = jnp.sum(jnp.where(hits, weights[:, :, :, None], 0.0), axis=2)
+    expert_in = jnp.einsum(
+        "btjc,btd->jbcd",
+        pick.astype(jnp.bfloat16).reshape(blocks, tok_rows, local_reps, capacity),
+        all_normed,
+        preferred_element_type=jnp.float32,
+    ).astype(jnp.bfloat16)
+    expert_in = expert_in.reshape(local_reps, blocks * capacity, model_width)
+    gate_up = jnp.einsum("jsd,jdf->jsf", expert_in, up_gate, preferred_element_type=jnp.float32)
+    hidden_act = (jax.nn.silu(gate_up[..., :hidden_units]) * gate_up[..., hidden_units:]).astype(
+        jnp.bfloat16
+    )
+    expert_out = jnp.einsum("jsf,jfd->jsd", hidden_act, down, preferred_element_type=jnp.float32)
+    expert_out = expert_out.astype(jnp.bfloat16).reshape(local_reps, blocks, capacity, model_width)
+    upper = slot_weight.astype(jnp.bfloat16)
+    lower = (slot_weight - upper.astype(jnp.float32)).astype(jnp.bfloat16)
+    split = jnp.stack([upper, lower]).reshape(2, blocks, tok_rows, local_reps, capacity)
+    twice = jnp.broadcast_to(expert_out[None], (2,) + expert_out.shape)
+    partial = jnp.einsum(
+        "hbtjc,hjbcd->btd", split, twice, preferred_element_type=jnp.float32
+    ).astype(jnp.bfloat16)
+    combined = lax.psum_scatter(partial, axes, scatter_dimension=0, tiled=False)
+    return (residual + combined.astype(jnp.float32)).astype(jnp.bfloat16)
+
+
 def solution(mesh):
+    device_count = mesh.shape["dp"] * mesh.shape["expert"]
+    plan = per_device_gathered if device_count <= 32 else per_device
     return jax.shard_map(
-        per_device,
+        plan,
         mesh=mesh,
         in_specs=(
             P(("dp", "expert"), None),

time: 521 us -> 542 us (1.040)
  waiting for transfers between devices: 76.2 us -> 266 us
  blocking collectives: 351 us -> 201 us
  local copies, waits for them, and re-layouts: 25.3 us -> 0.5 us
  matrix products: 38.4 us -> 52.6 us
    all_to_all x3 -> x0, blocking collectives: 200 us -> none  [the longest x1 97.4 us: per_device(): lax.all_to_all(outgoing, 'expert', split_axis=1, concat_axis=1, tiled=True)]
    reduce_scatter x0 -> x1, waiting for transfers between devices: none -> 183 us  [per_device_gathered(): combined = lax.psum_scatter(partial, axes, scatter_dimension=0, tiled=False)]
    all_gather x1 -> x3, blocking collectives: 151 us -> 201 us  [the longest x1 68 us: per_device_gathered(): positions = lax.all_gather(position, axes, axis=0, tiled=False)]
    gather x2 -> x0, local copies, waits for them, and re-layouts: 13.2 us -> none  [the longest x1 7.18 us: per_device(): gathered = returned[safe_index]]
    all_gather x1 -> x2, waiting for transfers between devices: 75.5 us -> 83.2 us  [the longest x1 83.1 us: per_device_gathered(): proj_rows = lax.all_gather(out_proj, axes, axis=0, tiled=True)]
    dot_general x4 -> x5, matrix products: 38.4 us -> 46 us  [the longest x1 18.3 us: per_device_gathered(): jnp.einsum('jsd,jdf->jsf', expert_in, up_gate, preferred_element_type=jnp...]
    all_to_all x3 -> x0, local copies, waits for them, and re-layouts: 7.6 us -> none  [the longest x1 4.75 us: per_device(): lax.all_to_all(lax.all_to_all(results, 'dp', split_axis=0, concat_axis=0,...]
    unnamed x0 -> x1, matrix products: none -> 6.59 us
  transfers between devices with their start and end apart: 2 -> 3, of which waited for: 1 -> 2; matrix products, arithmetic and copies ran while one was open for 2% -> 1% of each run, Pallas kernels for 0% -> 0%
where the time goes in v1:
time: 542 us
  waiting for transfers between devices  266 us (49%)
  blocking collectives  201 us (37%)
  matrix products  52.6 us (10%)
  between operations  13.3 us (2%)
  other arithmetic  7.94 us (1%)
    reduce_scatter x1, waiting for transfers between devices, per_device_gathered(): combined = lax.psum_scatter(partial, axes, scatter_dimension=0, tiled=False)  183 us
    all_gather x1, waiting for transfers between devices, per_device_gathered(): proj_rows = lax.all_gather(out_proj, axes, axis=0, tiled=True)  83.1 us
    all_gather x1, blocking collectives, per_device_gathered(): positions = lax.all_gather(position, axes, axis=0, tiled=False)  68 us
    all_gather x1, blocking collectives, per_device_gathered(): weights = lax.all_gather(route_weight, axes, axis=0, tiled=False)  66.4 us
    all_gather x1, blocking collectives, per_device_gathered(): router_rows = lax.all_gather(router, axes, axis=0, tiled=True)  66.4 us
    dot_general x1, matrix products, per_device_gathered(): jnp.einsum('jsd,jdf->jsf', expert_in, up_gate, preferred_element_type=jnp...  18.3 us
    dot_general x1, matrix products, per_device_gathered(): jnp.einsum('jsf,jfd->jsd', hidden_act, down, preferred_element_type=jnp.f...  15 us
  transfers between devices with their start and end apart: 3, of which 2 were waited for; matrix products, arithmetic and copies ran while one was open for 1% of the time, Pallas kernels for 0%

profile of v1, /device:TPU:0, one launch (start us, length us, event | category | flops | bytes accessed | tf_op | source)
XLA Modules:
  0.0 541.7 jit_solution(15114210386043356406)
XLA Ops:
  6.5 0.0 copy-start
  6.5 0.0 all-gather.4.cloned.1.call-start
  6.5 0.7 all-gather.4.cloned.1.call-update
  7.3 0.0 copy-start.3
  7.3 0.0 copy-start.4
  7.3 0.0 copy-start.5
  7.3 0.0 copy-start.6
  7.3 0.0 copy-start.2
  7.3 0.0 all-gather.6.cloned.1.call-start
  7.4 83.1 %all-gather.4.cloned.1.call-done = bf16[2048,2048]{1,0:T(8,128)(2,1)} async-done(((bf16[64,2048]{1,0:T(8,128)(2,1)}), bf16[2048,2048]{1,0:T(8,128)(2,1)}) %all-gather.4.cloned.1.call-update) | async-done | bytes 8388624 | tf_op jit(solution)/shard_map/all_gather | solution.py:131
  90.5 0.0 copy-done
  90.5 5.1 multiply_reduce_fusion
  95.6 0.0 copy-done.3
  95.6 0.8 multiply_convert_fusion
  96.4 0.0 all-gather.6.cloned.1.call-update
  96.4 0.0 reduce-scatter.2.cloned.1.call-start
  96.5 0.0 copy-done.4
  96.5 0.1 copy.28
  96.6 0.0 copy-done.5
  96.6 0.1 copy.29
  96.7 0.0 copy-done.6
  96.7 0.2 convert_reduce_fusion.1
  96.9 1.2 fusion.15
  98.1 0.4 add_select_fusion
  98.5 1.3 select_reduce_fusion.2
  99.8 0.1 eq.94
  99.9 0.3 convert_reduce_fusion
  100.1 0.1 reshape.126
  100.3 0.1 copy.30
  100.3 68.0 %all_gather.21 = s32[32,64,8]{1,2,0:T(8,128)S(1)} all-gather(s32[1,64,8]{1,2,0:T(8,128)S(1)} %copy.30), channel_id=1, replica_groups=mesh['dp'=4,'expert'=8] {'dp','expert'}, dimensions={0}, use_global_device_ids=true | all-gather | bytes 67584 | tf_op jit(solution)/shard_map/all_gather | solution.py:135
  168.3 66.4 %all_gather.22 = bf16[2048,64]{1,0:T(8,128)(2,1)S(1)} all-gather(bf16[64,64]{1,0:T(8,128)(2,1)S(1)} %copy-done.2), channel_id=1, replica_groups=mesh['dp'=4,'expert'=8] {'dp','expert'}, dimensions={0}, use_global_device_ids=true | all-gather | bytes 270336 | tf_op jit(solution)/shard_map/all_gather | solution.py:132
  234.7 0.7 fusion.5
  235.3 1.2 fusion.20
  236.5 0.2 select_reduce_fusion.1
  236.7 0.1 exponential_reduce_fusion
  236.8 0.1 bitcast_divide_fusion
  236.9 0.1 copy.32
  237.0 66.4 %all_gather.23 = f32[32,64,8]{1,2,0:T(8,128)S(1)} all-gather(f32[1,64,8]{1,2,0:T(8,128)S(1)} %copy.32), channel_id=1, replica_groups=mesh['dp'=4,'expert'=8] {'dp','expert'}, dimensions={0}, use_global_device_ids=true | all-gather | bytes 67584 | tf_op jit(solution)/shard_map/all_gather | solution.py:145
  303.4 0.9 select_reduce_fusion
  304.3 0.1 fusion.14
  304.4 0.0 all-gather.6.cloned.1.call-done
  304.4 6.6 %fusion.6 = bf16[4,32,8,2048]{3,2,0,1:T(8,128)(2,1)} fusion(bf16[32,64,2048]{2,1,0:T(8,128)(2,1)} %bitcast.42, pred[32,64,32]{1,2,0:T(8,128)(4,1)S(1)} %fusion.5), kind=kOutput, calls=%fused_computation.12 | convolution fusion | flops 270532608 | bytes 12648448
  311.0 18.3 %fusion.1 = f32[4,256,2048]{2,1,0:T(8,128)} fusion(bf16[4,2048,2048]{2,1,0:T(8,128)(2,1)} %param.18, bf16[4,32,8,2048]{3,2,0,1:T(8,128)(2,1)} %fusion.6), kind=kOutput, calls=%fused_computation.4 | convolution fusion | flops 8589934592 | bytes 46137344 | tf_op jit(solution)/shard_map/jsd,jdf->jsf/dot_general | solution.py:157
  329.3 15.0 %convert_bitcast_fusion = bf16[4,32,8,2048]{3,2,1,0:T(8,128)(2,1)} fusion(bf16[4,1024,2048]{2,1,0:T(8,128)(2,1)} %param.19, f32[4,256,2048]{2,1,0:T(8,128)} %fusion.1), kind=kOutput, calls=%fused_computation.8 | convolution fusion | flops 4303355904 | bytes 29360128 | tf_op jit(solution)/shard_map/jsf,jfd->jsd/dot_general | solution.py:161
  344.3 6.6 %bitcast_convert_fusion = bf16[32,64,2048]{2,1,0:T(8,128)(2,1)} fusion(bf16[1,32,64,4,8]{2,4,3,1,0:T(8,128)(2,1)S(1)} %get-tuple-element.5, bf16[1,32,64,4,8]{2,4,3,1,0:T(8,128)(2,1)S(1)} %get-tuple-element.6, bf16[4,32,8,2048]{3,2,1,0:T(8,128)(2,1)} %convert_bitcast_fusion), kind=kOutput, calls=%fused_computation | convolution fusion | flops 541196288 | bytes 12845056 | tf_op jit(solution)/shard_map/hbtjc,hjbcd->btd/dot_general | solution.py:167
  350.8 0.0 reduce-scatter.2.cloned.1.call-update
  350.9 182.6 %reduce-scatter.2.cloned.1.call-done = bf16[1,64,2048]{2,1,0:T(8,128)(2,1)} async-done(((bf16[32,64,2048]{2,1,0:T(8,128)(2,1)}), bf16[1,64,2048]{2,1,0:T(8,128)(2,1)}) %reduce-scatter.2.cloned.1.call-update) | async-done | bytes 262160 | tf_op jit(solution)/shard_map/reduce_scatter | solution.py:170
  533.4 1.7 fusion.13
  (6 shorter events, 0.0 us)
Async XLA Ops:
  6.5 84.0 %copy-start = (bf16[64,2048]{1,0:T(8,128)(2,1)S(1)}, bf16[64,2048]{1,0:T(8,128)(2,1)}, u32[]{:S(2)}) copy-start(bf16[64,2048]{1,0:T(8,128)(2,1)} %param.11) | copy-start | bytes 786436
  6.5 84.0 %all-gather.4.cloned.1.call-start = ((), (), s32[]{:S(2)}) async-start(), calls=%async_computation.1 | async-start | bytes 8650752 | tf_op jit(solution)/shard_map/all_gather | solution.py:131
  7.3 88.3 %copy-start.3 = (f32[2048]{0:T(1024)S(1)}, f32[2048]{0:T(1024)}, u32[]{:S(2)}) copy-start(f32[2048]{0:T(1024)} %param.13) | copy-start | bytes 24580
  7.3 89.2 %copy-start.4 = (s32[64,8]{0,1:T(8,128)S(1)}, s32[64,8]{0,1:T(8,128)}, u32[]{:S(2)}) copy-start(s32[64,8]{0,1:T(8,128)} %param.15) | copy-start | bytes 6148
  7.3 89.3 %copy-start.5 = (s32[64,8]{0,1:T(8,128)S(1)}, s32[64,8]{0,1:T(8,128)}, u32[]{:S(2)}) copy-start(s32[64,8]{0,1:T(8,128)} %param.17) | copy-start | bytes 6148
  7.3 89.4 %copy-start.6 = (s32[128]{0:T(128)S(1)}, s32[128]{0:T(128)}, u32[]{:S(2)}) copy-start(s32[128]{0:T(128)} %param.16) | copy-start | bytes 1540
  7.3 161.0 %copy-start.2 = (bf16[64,64]{1,0:T(8,128)(2,1)S(1)}, bf16[64,64]{1,0:T(8,128)(2,1)}, u32[]{:S(2)}) copy-start(bf16[64,64]{1,0:T(8,128)(2,1)} %param.14) | copy-start | bytes 24580
  7.3 297.1 %all-gather.6.cloned.1.call-start = ((), (), s32[]{:S(2)}) async-start(), calls=%async_computation.3 | async-start | bytes 8650752 | tf_op jit(solution)/shard_map/all_gather | solution.py:139
  96.4 437.0 %reduce-scatter.2.cloned.1.call-start = ((), (), s32[]{:S(2)}) async-start(), calls=%async_computation.2 | async-start | bytes 8650752 | tf_op jit(solution)/shard_map/reduce_scatter | solution.py:170
  350.8 184.3 %copy-start.1 = (bf16[64,2048]{1,0:T(8,128)(2,1)S(1)}, bf16[64,2048]{1,0:T(8,128)(2,1)}, u32[]{:S(2)}) copy-start(bf16[64,2048]{1,0:T(8,128)(2,1)} %param.11) | copy-start | bytes 786436
Sparse Core Ops, SparseCore 0:
  10.3 80.1 all-gather.3
  96.6 77.7 all-gather.5
  351.0 182.3 reduce-scatter.1

commit v2 on v1

--- a/solution.py
+++ b/solution.py
@@ -1,6 +1,10 @@
+import functools
+
 import jax
 import jax.numpy as jnp
 from jax import lax
+from jax.experimental import pallas as pl
+from jax.experimental.pallas import tpu as pltpu
 from jax.sharding import PartitionSpec as P
 
 
@@ -105,6 +109,353 @@
     layer_out = residual + jnp.sum(kept_weight[:, :, None] * gathered.astype(jnp.float32), axis=1)
     return layer_out.astype(jnp.bfloat16)
 
+MESH = pl.DeviceIdType.MESH
+
+
+def place():
+    d, e = lax.axis_index("dp"), lax.axis_index("expert")
+    return d // 2, d % 2, e // 2, e % 2
+
+
+def device_of(y, c, z, x):
+    return (y * 2 + c, z * 2 + x)
+
+
+def block_of(y, c, z, x):
+    return (y * 2 + c) * (2 * LINE) + z * 2 + x
+
+
+LINE = 4
+
+
+def greet(barrier, y, c, z, x):
+    for other in (device_of(y, 1 - c, z, x), device_of(1 - y, c, z, x), device_of(y, c, z, 1 - x)):
+        pl.semaphore_signal(barrier, inc=1, device_id=other, device_id_type=MESH)
+
+    @pl.when(z > 0)
+    def _():
+        pl.semaphore_signal(barrier, inc=1, device_id=device_of(y, c, z - 1, x), device_id_type=MESH)
+
+    @pl.when(z < LINE - 1)
+    def _():
+        pl.semaphore_signal(barrier, inc=1, device_id=device_of(y, c, z + 1, x), device_id_type=MESH)
+
+    pl.semaphore_wait(barrier, 3 + jnp.minimum(z, 1) + jnp.minimum(LINE - 1 - z, 1))
+
+
+def gather_kernel(half, in_ref, out_ref, own_sem, line_sem, x_sem, y_sem, core_sem, recv_sem):
+    y, c, z, x = place()
+    greet(pltpu.get_barrier_semaphore(), y, c, z, x)
+    me = block_of(y, c, z, x)
+    up, down = device_of(y, c, z + 1, x), device_of(y, c, z - 1, x)
+    over_x, over_y = device_of(y, c, z, 1 - x), device_of(1 - y, c, z, x)
+    twin = device_of(y, 1 - c, z, x)
+
+    def piece(block, h):
+        return out_ref.at[block, pl.ds(h * half, half)]
+
+    def send(block, h, target, sem, own=False):
+        return pltpu.make_async_remote_copy(
+            src_ref=in_ref.at[pl.ds(h * half, half)] if own else piece(block, h),
+            dst_ref=piece(block, h),
+            send_sem=sem,
+            recv_sem=recv_sem.at[block, h],
+            device_id=target,
+            device_id_type=MESH,
+        )
+
+    def arrive(block, h):
+        send(block, h, twin, core_sem.at[0, 0]).wait_recv()
+
+    local = pltpu.make_async_copy(in_ref, out_ref.at[me], own_sem)
+    local.start()
+
+    def spread(source_z, own, going, act):
+        block = block_of(y, c, source_z, x)
+        for h in range(2):
+            if going >= 0:
+                @pl.when(z < LINE - 1)
+                def _():
+                    act(send(block, h, up, line_sem.at[0, source_z, h], own))
+            if going <= 0:
+                @pl.when(z > 0)
+                def _():
+                    act(send(block, h, down, line_sem.at[1, source_z, h], own))
+        for h in range(2):
+            act(send(block, h, over_x, x_sem.at[source_z, h], own))
+            act(send(block, 1 - h, over_y, y_sem.at[source_z, 1 - h], own))
+        for h in range(2):
+            act(send(block, h, twin, core_sem.at[source_z, h], own))
+
+    def hand_on(source_z, act, wait):
+        from_x = block_of(y, c, source_z, 1 - x)
+        from_y = block_of(1 - y, c, source_z, x)
+        if wait:
+            arrive(from_x, 0)
+        act(send(from_x, 0, over_y, y_sem.at[source_z, 2]))
+        act(send(from_x, 0, twin, core_sem.at[LINE + source_z, 0]))
+        if wait:
+            arrive(from_y, 1)
+        act(send(from_y, 1, over_x, x_sem.at[source_z, 2]))
+        act(send(from_y, 1, twin, core_sem.at[2 * LINE + source_z, 1]))
+        if wait:
+            arrive(from_x, 1)
+        act(send(from_x, 1, twin, core_sem.at[LINE + source_z, 1]))
+        if wait:
+            arrive(from_y, 0)
+        act(send(from_y, 0, twin, core_sem.at[2 * LINE + source_z, 0]))
+
+    def last_leg(source_z, act, wait):
+        across = block_of(1 - y, c, source_z, 1 - x)
+        for h in range(2):
+            if wait:
+                arrive(across, h)
+            act(send(across, h, twin, core_sem.at[3 * LINE + source_z, h]))
+
+    def start(copy):
+        copy.start()
+
+    def drain(copy):
+        copy.wait_send()
+
+    def by_distance(k, step):
+        @pl.when(z >= k)
+        def _():
+            step(z - k, 1)
+
+        @pl.when(z + k < LINE)
+        def _():
+            step(z + k, -1)
+
+    def come_along_z(source_z, going):
+        for h in range(2):
+            arrive(block_of(y, c, source_z, x), h)
+        spread(source_z, False, going, start)
+
+    spread(z, True, 0, start)
+    by_distance(1, come_along_z)
+    hand_on(z, start, True)
+    by_distance(2, come_along_z)
+    by_distance(1, lambda source_z, going: hand_on(source_z, start, True))
+    by_distance(3, come_along_z)
+    last_leg(z, start, True)
+    by_distance(2, lambda source_z, going: hand_on(source_z, start, True))
+    by_distance(1, lambda source_z, going: last_leg(source_z, start, True))
+    by_distance(3, lambda source_z, going: hand_on(source_z, start, True))
+    by_distance(2, lambda source_z, going: last_leg(source_z, start, True))
+    by_distance(3, lambda source_z, going: last_leg(source_z, start, True))
+    for other_y in range(2):
+        for other_x in range(2):
+            for source_z in range(LINE):
+                for h in range(2):
+                    arrive(block_of(other_y, 1 - c, source_z, other_x), h)
+    spread(z, True, 0, drain)
+    for k in range(1, LINE):
+        by_distance(k, lambda source_z, going: spread(source_z, False, going, drain))
+    for source_z in range(LINE):
+        hand_on(source_z, drain, False)
+        last_leg(source_z, drain, False)
+    local.wait()
+
+
+def gather_rows(array, collective_id):
+    rows, width = array.shape
+    blocks = 8 * LINE
+    dma = pltpu.SemaphoreType.DMA
+    return pl.pallas_call(
+        functools.partial(gather_kernel, rows // 2),
+        out_shape=jax.ShapeDtypeStruct((blocks, rows, width), array.dtype),
+        in_specs=[pl.BlockSpec(memory_space=pl.ANY)],
+        out_specs=pl.BlockSpec(memory_space=pl.ANY),
+        scratch_shapes=[
+            dma,
+            dma((2, LINE, 2)),
+            dma((LINE, 3)),
+            dma((LINE, 3)),
+            dma((4 * LINE, 2)),
+            dma((blocks, 2)),
+        ],
+        compiler_params=pltpu.CompilerParams(collective_id=collective_id, has_side_effects=True),
+    )(array)
+
+
+def scatter_kernel(half, in_ref, out_ref, core_buf, x_buf, y_buf, diag_buf, line_buf, core_sem, x_sem, y_sem,
+                   line_sem, core_recv, x_recv, y_recv, diag_recv, line_recv):
+    y, c, z, x = place()
+    greet(pltpu.get_barrier_semaphore(), y, c, z, x)
+    up, down = device_of(y, c, z + 1, x), device_of(y, c, z - 1, x)
+    over_x, over_y = device_of(y, c, z, 1 - x), device_of(1 - y, c, z, x)
+    twin = device_of(y, 1 - c, z, x)
+
+    def block(quadrant, target_z, core):
+        return block_of(*((1 - y) if quadrant >= 2 else y, core, target_z, (1 - x) if quadrant % 2 else x))
+
+    def part(h):
+        return pl.ds(h * half, half)
+
+    def remote(src, dst, send_sem, recv_sem, target):
+        return pltpu.make_async_remote_copy(
+            src_ref=src, dst_ref=dst, send_sem=send_sem, recv_sem=recv_sem, device_id=target, device_id_type=MESH
+        )
+
+    def to_core(q, tz, h):
+        return remote(
+            in_ref.at[block(q, tz, 1 - c), part(h)],
+            core_buf.at[q, tz, part(h)],
+            core_sem.at[q, tz, h],
+            core_recv.at[q, tz, h],
+            twin,
+        )
+
+    def across(tz, h):
+        return remote(
+            core_buf.at[3, tz, part(h)],
+            diag_buf.at[h, tz],
+            (y_sem if h == 0 else x_sem).at[tz, 2],
+            diag_recv.at[h, tz],
+            over_y if h == 0 else over_x,
+        )
+
+    def to_x(tz, h):
+        return remote(core_buf.at[1, tz, part(h)], x_buf.at[tz, part(h)], x_sem.at[tz, h], x_recv.at[tz, h], over_x)
+
+    def to_y(tz, h):
+        return remote(core_buf.at[2, tz, part(h)], y_buf.at[tz, part(h)], y_sem.at[tz, h], y_recv.at[tz, h], over_y)
+
+    def along(way, tz):
+        return remote(
+            core_buf.at[0, tz], line_buf.at[way, tz], line_sem.at[way, tz], line_recv.at[way, tz],
+            up if way == 0 else down,
+        )
+
+    def add_into(target, source):
+        target[...] = (target[...].astype(jnp.float32) + source[...].astype(jnp.float32)).astype(target.dtype)
+
+    def add_core(q, tz, h):
+        to_core(q, tz, h).wait_recv()
+        add_into(core_buf.at[q, tz, part(h)], in_ref.at[block(q, tz, c), part(h)])
+
+    def through(tz):
+        for h in range(2):
+            add_core(3, tz, h)
+            across(tz, h).start()
+        add_core(1, tz, 1)
+        to_x(tz, 1).start()
+        add_core(2, tz, 0)
+        to_y(tz, 0).start()
+        add_core(1, tz, 0)
+        across(tz, 0).wait_recv()
+        add_into(core_buf.at[1, tz, part(0)], diag_buf.at[0, tz])
+        to_x(tz, 0).start()
+        add_core(2, tz, 1)
+        across(tz, 1).wait_recv()
+        add_into(core_buf.at[2, tz, part(1)], diag_buf.at[1, tz])
+        to_y(tz, 1).start()
+        for h in range(2):
+            add_core(0, tz, h)
+
+    def collect(tz):
+        for h in (1, 0):
+            to_x(tz, h).wait_recv()
+            add_into(core_buf.at[0, tz, part(h)], x_buf.at[tz, part(h)])
+        for h in (0, 1):
+            to_y(tz, h).wait_recv()
+            add_into(core_buf.at[0, tz, part(h)], y_buf.at[tz, part(h)])
+
+    def by_distance(k, step):
+        @pl.when(z + k < LINE)
+        def _():
+            step(z + k, 0)
+
+        @pl.when(z >= k)
+        def _():
+            step(z - k, 1)
+
+    def pass_on(tz, way):
+        collect(tz)
+
+        @pl.when((z > 0) if way == 0 else (z < LINE - 1))
+        def _():
+            along(way, tz).wait_recv()
+            add_into(core_buf.at[0, tz], line_buf.at[way, tz])
+
+        along(way, tz).start()
+
+    for k in (3, 2, 1, 0):
+        def offer(tz, way):
+            for q in (3, 1, 2, 0):
+                for h in ((1, 0) if q == 1 else (0, 1)):
+                    to_core(q, tz, h).start()
+
+        if k:
+            by_distance(k, offer)
+        else:
+            offer(z, 0)
+    by_distance(3, lambda tz, way: through(tz))
+    by_distance(2, lambda tz, way: through(tz))
+    by_distance(3, pass_on)
+    by_distance(1, lambda tz, way: through(tz))
+    by_distance(2, pass_on)
+    through(z)
+    by_distance(1, pass_on)
+    collect(z)
+
+    @pl.when(z > 0)
+    def _():
+        along(0, z).wait_recv()
+        add_into(core_buf.at[0, z], line_buf.at[0, z])
+
+    @pl.when(z < LINE - 1)
+    def _():
+        along(1, z).wait_recv()
+        add_into(core_buf.at[0, z], line_buf.at[1, z])
+
+    out_ref[...] = core_buf[0, z]
+    for tz in range(LINE):
+        for q in range(4):
+            for h in range(2):
+                to_core(q, tz, h).wait_send()
+        for h in range(2):
+            across(tz, h).wait_send()
+            to_x(tz, h).wait_send()
+            to_y(tz, h).wait_send()
+    for k in (1, 2, 3):
+        by_distance(k, lambda tz, way: along(way, tz).wait_send())
+
+
+def scatter_sum(partial, collective_id):
+    blocks, rows, width = partial.shape
+    half = rows // 2
+    dma = pltpu.SemaphoreType.DMA
+    return pl.pallas_call(
+        functools.partial(scatter_kernel, half),
+        out_shape=jax.ShapeDtypeStruct((rows, width), partial.dtype),
+        in_specs=[pl.BlockSpec(memory_space=pltpu.VMEM)],
+        out_specs=pl.BlockSpec(memory_space=pltpu.VMEM),
+        scratch_shapes=[
+            pltpu.VMEM((4, LINE, rows, width), partial.dtype),
+            pltpu.VMEM((LINE, rows, width), partial.dtype),
+            pltpu.VMEM((LINE, rows, width), partial.dtype),
+            pltpu.VMEM((2, LINE, half, width), partial.dtype),
+            pltpu.VMEM((2, LINE, rows, width), partial.dtype),
+            dma((4, LINE, 2)),
+            dma((LINE, 3)),
+            dma((LINE, 3)),
+            dma((2, LINE)),
+            dma((4, LINE, 2)),
+            dma((LINE, 2)),
+            dma((LINE, 2)),
+            dma((2, LINE)),
+            dma((2, LINE)),
+        ],
+        compiler_params=pltpu.CompilerParams(
+            collective_id=collective_id, has_side_effects=True, vmem_limit_bytes=48 << 20
+        ),
+    )(partial)
+
+
+SIDE = 128
+
 
 def per_device_gathered(
     hidden_in,
@@ -118,8 +469,8 @@
     up_gate,
     down,
 ):
-    axes = ("dp", "expert")
     tok_rows, model_width = hidden_in.shape
+    expert_total = router.shape[1]
     top_count = expert_ids.shape[1]
     replica_total = replica_expert.shape[0]
     local_reps = up_gate.shape[0]
@@ -128,52 +479,62 @@
     me = lax.axis_index("dp") * lax.axis_size("expert") + lax.axis_index("expert")
     capacity = max(2, 2 * tok_rows * top_count // replica_total)
     local_slots = local_reps * capacity
-    proj_rows = lax.all_gather(out_proj, axes, axis=0, tiled=True)
-    router_rows = lax.all_gather(router, axes, axis=0, tiled=True)
+    side = jnp.pad(router, ((0, 0), (0, SIDE - expert_total)))
+    proj_rows = gather_rows(jnp.concatenate([out_proj, side], axis=1), 0)
+    proj_rows = proj_rows.reshape(blocks * out_proj.shape[0], model_width + SIDE)
+    router_rows = proj_rows[:, model_width : model_width + expert_total]
     replica, slot_index = route_block(expert_ids, split_pick, replica_expert)
-    position = jnp.where(slot_index < capacity, replica * capacity + slot_index, -1)
-    positions = lax.all_gather(position, axes, axis=0, tiled=False)
-    summed = jnp.dot(context, proj_rows, preferred_element_type=jnp.float32)
+    slot_index = jnp.minimum(slot_index, capacity)
+    summed = jnp.dot(context, proj_rows, preferred_element_type=jnp.float32)[:, :model_width]
     residual = hidden_in.astype(jnp.float32) + summed
     normed = rms_norm(residual, norm_gain)
-    all_normed = lax.all_gather(normed, axes, axis=0, tiled=False)
     logits = jnp.dot(normed, router_rows, preferred_element_type=jnp.float32)
-    hit_mask = expert_ids[:, :, None] == lax.iota(jnp.int32, logits.shape[1])[None, None, :]
+    hit_mask = expert_ids[:, :, None] == lax.iota(jnp.int32, expert_total)[None, None, :]
     chosen = jnp.sum(jnp.where(hit_mask, logits[:, None, :], 0.0), axis=-1)
     raised = jnp.exp(chosen)
     route_weight = raised / jnp.sum(raised, axis=-1, keepdims=True)
-    weights = lax.all_gather(route_weight, axes, axis=0, tiled=False)
-    local_iota = lax.iota(jnp.int32, local_slots)
-    hits = (positions - me * local_slots)[:, :, :, None] == local_iota
-    pick = jnp.any(hits, axis=2)
-    slot_weight = jnp.sum(jnp.where(hits, weights[:, :, :, None], 0.0), axis=2)
+    upper = route_weight.astype(jnp.bfloat16)
+    lower = (route_weight - upper.astype(jnp.float32)).astype(jnp.bfloat16)
+    side = jnp.concatenate(
+        [upper, lower, replica.astype(jnp.bfloat16), slot_index.astype(jnp.bfloat16)], axis=1
+    )
+    side = jnp.pad(side, ((0, 0), (0, SIDE - 4 * top_count)))
+    all_rows = gather_rows(jnp.concatenate([normed, side], axis=1), 1)
+    side = all_rows[:, :, model_width : model_width + 4 * top_count]
+    upper, lower, replica, slot_index = [
+        side[:, :, part * top_count : (part + 1) * top_count] for part in range(4)
+    ]
+    replica = replica.astype(jnp.int32) - me * local_reps
+    slot_index = slot_index.astype(jnp.int32)
+    place_here = jnp.where(slot_index < capacity, replica * capacity + slot_index, -1)
+    hits = place_here[:, :, :, None] == lax.iota(jnp.int32, local_slots)
+    pick = jnp.any(hits, axis=2).astype(jnp.bfloat16)
+    upper = jnp.sum(jnp.where(hits, upper[:, :, :, None], 0), axis=2)
+    lower = jnp.sum(jnp.where(hits, lower[:, :, :, None], 0), axis=2)
     expert_in = jnp.einsum(
         "btjc,btd->jbcd",
-        pick.astype(jnp.bfloat16).reshape(blocks, tok_rows, local_reps, capacity),
-        all_normed,
+        pick.reshape(blocks, tok_rows, local_reps, capacity),
+        all_rows,
         preferred_element_type=jnp.float32,
     ).astype(jnp.bfloat16)
-    expert_in = expert_in.reshape(local_reps, blocks * capacity, model_width)
+    expert_in = expert_in[..., :model_width].reshape(local_reps, blocks * capacity, model_width)
     gate_up = jnp.einsum("jsd,jdf->jsf", expert_in, up_gate, preferred_element_type=jnp.float32)
     hidden_act = (jax.nn.silu(gate_up[..., :hidden_units]) * gate_up[..., hidden_units:]).astype(
         jnp.bfloat16
     )
     expert_out = jnp.einsum("jsf,jfd->jsd", hidden_act, down, preferred_element_type=jnp.float32)
     expert_out = expert_out.astype(jnp.bfloat16).reshape(local_reps, blocks, capacity, model_width)
-    upper = slot_weight.astype(jnp.bfloat16)
-    lower = (slot_weight - upper.astype(jnp.float32)).astype(jnp.bfloat16)
     split = jnp.stack([upper, lower]).reshape(2, blocks, tok_rows, local_reps, capacity)
     twice = jnp.broadcast_to(expert_out[None], (2,) + expert_out.shape)
     partial = jnp.einsum(
         "hbtjc,hjbcd->btd", split, twice, preferred_element_type=jnp.float32
     ).astype(jnp.bfloat16)
-    combined = lax.psum_scatter(partial, axes, scatter_dimension=0, tiled=False)
+    combined = scatter_sum(partial, 2)
     return (residual + combined.astype(jnp.float32)).astype(jnp.bfloat16)
 
 
 def solution(mesh):
-    device_count = mesh.shape["dp"] * mesh.shape["expert"]
-    plan = per_device_gathered if device_count <= 32 else per_device
+    plan = per_device_gathered if (mesh.shape["dp"], mesh.shape["expert"]) == (4, 8) else per_device
     return jax.shard_map(
         plan,
         mesh=mesh,

time: 542 us -> 206 us (0.38)
  waiting for transfers between devices: 266 us -> 0 us
  blocking collectives: 201 us -> 0 us
  Pallas kernels: 0 us -> 134 us
  between operations: 13.3 us -> 0.17 us
  other arithmetic: 7.94 us -> 13.4 us
    all_gather x3 -> x0, blocking collectives: 201 us -> none  [the longest x1 68 us: per_device_gathered(): positions = lax.all_gather(position, axes, axis=0, tiled=False)]
    reduce_scatter x1 -> x0, waiting for transfers between devices: 183 us -> none  [per_device_gathered(): combined = lax.psum_scatter(partial, axes, scatter_dimension=0, tiled=False)]
    pallas_call x0 -> x3, Pallas kernels: none -> 134 us  [the longest x2 89.8 us: gather_rows(): pl.pallas_call(functools.partial(gather_kernel, rows // 2), out_shape=jax...]
    all_gather x2 -> x0, waiting for transfers between devices: 83.2 us -> none  [the longest x1 83.1 us: per_device_gathered(): proj_rows = lax.all_gather(out_proj, axes, axis=0, tiled=True)]
  transfers between devices with their start and end apart: 3 -> 0, of which waited for: 2 -> 0; matrix products, arithmetic and copies ran while one was open for 1% -> 0% of each run, Pallas kernels for 0% -> 0%
where the time goes in v2:
time: 206 us
  Pallas kernels  134 us (65%)
  matrix products  53.4 us (26%)
  other arithmetic  13.4 us (7%)
  local copies, waits for them, and re-layouts  4.19 us (2%)
    pallas_call x2, Pallas kernels, gather_rows(): pl.pallas_call(functools.partial(gather_kernel, rows // 2), out_shape=jax...  89.8 us
    pallas_call x1, Pallas kernels, scatter_sum(): pl.pallas_call(functools.partial(scatter_kernel, half), out_shape=jax.Sha...  44.7 us
    dot_general x1, matrix products, per_device_gathered(): jnp.einsum('jsd,jdf->jsf', expert_in, up_gate, preferred_element_type=jnp...  18.3 us
    dot_general x1, matrix products, per_device_gathered(): jnp.einsum('jsf,jfd->jsd', hidden_act, down, preferred_element_type=jnp.f...  15 us
    unnamed x1, matrix products  7.06 us
    dot_general x1, matrix products, per_device_gathered(): jnp.einsum('hbtjc,hjbcd->btd', split, twice, preferred_element_type=jnp.f...  6.61 us
    dot_general x1, matrix products, per_device_gathered(): jnp.dot(context, proj_rows, preferred_element_type=jnp.float32)  5.2 us

profile of v2, /device:TPU:0, one launch (start us, length us, event | category | flops | bytes accessed | tf_op | source)
XLA Modules:
  0.0 205.6 jit_solution(4965920499651667732)
XLA Ops:
  0.0 0.0 copy-start
  0.0 0.8 copy.32
  0.8 0.8 copy.28
  1.6 1.9 fusion.22
  3.5 0.4 add_select_fusion
  3.9 0.9 convert_reduce_fusion.1
  4.8 2.0 select_reduce_fusion
  6.7 0.1 eq.97
  6.8 0.3 convert_reduce_fusion
  7.1 0.1 convert_element_type.82
  7.2 1.7 fusion.21.in_ref
  8.9 45.6 %shard_map.100 = bf16[32,64,2176]{2,1,0:T(8,128)(2,1)} custom-call(bf16[64,2176]{1,0:T(8,128)(2,1)} %fusion.21.in_ref), custom_call_target="tpu_custom_call" | custom-call | tf_op jit(solution)/shard_map/pallas_call | solution.py:265
  54.5 0.0 copy-done
  54.5 0.0 copy-start.2
  54.5 0.0 copy-start.3
  54.5 5.2 %convolution_bitcast_fusion = f32[64,2176]{1,0:T(8,128)S(1)} fusion(bf16[64,2048]{1,0:T(8,128)(2,1)S(1)} %copy-done, bf16[2048,2176]{1,0:T(8,128)(2,1)} %bitcast.30), kind=kOutput, calls=%fused_computation.14 | convolution fusion | flops 570425344 | bytes 9732096 | tf_op jit(solution)/shard_map/dot_general | solution.py:488
  59.7 0.0 copy-done.2
  59.7 0.2 multiply_reduce_fusion
  59.9 0.0 copy-done.3
  59.9 0.1 multiply_convert_fusion
  60.1 1.3 fusion.16
  61.3 0.2 select_reduce_fusion.1
  61.6 0.1 copy.29
  61.6 0.1 copy.30
  61.7 0.1 fusion.31
  61.8 0.1 fusion.30
  61.9 0.7 pad_maximum_fusion.in_ref
  62.7 44.2 %shard_map.101 = bf16[32,64,2176]{2,1,0:T(8,128)(2,1)} custom-call(bf16[64,2176]{1,0:T(8,128)(2,1)} %pad_maximum_fusion.in_ref), custom_call_target="tpu_custom_call" | custom-call | tf_op jit(solution)/shard_map/pallas_call | solution.py:265
  106.9 1.8 fusion.13
  108.7 0.3 copy.33
  109.0 1.5 fusion.34
  110.6 0.2 copy.34
  110.8 0.2 copy.35
  111.0 1.6 fusion.9
  112.6 0.7 fusion.6
  113.2 7.1 %fusion = bf16[4,32,8,2176]{3,2,0,1:T(8,128)(2,1)} fusion(bf16[32,64,2176]{2,1,0:T(8,128)(2,1)} %shard_map.101, pred[32,64,32]{1,2,0:T(8,128)(4,1)S(1)} %fusion.6), kind=kOutput, calls=%fused_computation.2 | convolution fusion | flops 287440896 | bytes 13434880
  120.3 18.3 %fusion.2 = f32[4,256,2048]{2,1,0:T(8,128)} fusion(bf16[4,2048,2048]{2,1,0:T(8,128)(2,1)} %param.18, bf16[4,32,8,2176]{3,2,0,1:T(8,128)(2,1)} %fusion), kind=kOutput, calls=%fused_computation.5 | convolution fusion | flops 8589934592 | bytes 46137344 | tf_op jit(solution)/shard_map/jsd,jdf->jsf/dot_general | solution.py:521
  138.5 15.0 %convert_bitcast_fusion = bf16[4,32,8,2048]{3,2,1,0:T(8,128)(2,1)} fusion(bf16[4,1024,2048]{2,1,0:T(8,128)(2,1)} %param.19, f32[4,256,2048]{2,1,0:T(8,128)} %fusion.2), kind=kOutput, calls=%fused_computation.9 | convolution fusion | flops 4303355904 | bytes 29360128 | tf_op jit(solution)/shard_map/jsf,jfd->jsd/dot_general | solution.py:525
  153.5 0.0 copy-start.1
  153.5 6.6 %bitcast_convert_fusion.in_ref = bf16[32,64,2048]{2,1,0:T(8,128)(2,1)} fusion(bf16[1,32,64,4,8]{2,4,3,1,0:T(8,128)(2,1)S(1)} %bitcast.33, bf16[1,32,64,4,8]{2,4,3,1,0:T(8,128)(2,1)S(1)} %bitcast.32, bf16[4,32,8,2048]{3,2,1,0:T(8,128)(2,1)} %convert_bitcast_fusion), kind=kOutput, calls=%fused_computation | convolution fusion | flops 541196288 | bytes 12845056 | tf_op jit(solution)/shard_map/hbtjc,hjbcd->btd/dot_general | solution.py:529
  160.1 44.7 %shard_map.102 = bf16[64,2048]{1,0:T(8,128)(2,1)S(1)} custom-call(bf16[32,64,2048]{2,1,0:T(8,128)(2,1)} %bitcast_convert_fusion.in_ref), custom_call_target="tpu_custom_call" | custom-call | tf_op jit(solution)/shard_map/pallas_call | solution.py:430
  204.8 0.8 add_convert_fusion
  205.6 0.0 copy-done.1
  (4 shorter events, 0.0 us)
Async XLA Ops:
  0.0 54.5 %copy-start = (bf16[64,2048]{1,0:T(8,128)(2,1)S(1)}, bf16[64,2048]{1,0:T(8,128)(2,1)}, u32[]{:S(2)}) copy-start(bf16[64,2048]{1,0:T(8,128)(2,1)} %param.11) | copy-start | bytes 786436
  54.5 5.2 %copy-start.2 = (bf16[64,2048]{1,0:T(8,128)(2,1)S(1)}, bf16[64,2048]{1,0:T(8,128)(2,1)}, u32[]{:S(2)}) copy-start(bf16[64,2048]{1,0:T(8,128)(2,1)} %param.10) | copy-start | bytes 786436
  54.5 5.4 %copy-start.3 = (f32[2048]{0:T(1024)S(1)}, f32[2048]{0:T(1024)}, u32[]{:S(2)}) copy-start(f32[2048]{0:T(1024)} %param.13) | copy-start | bytes 24580
  153.5 52.1 %copy-start.1 = (bf16[64,2048]{1,0:T(8,128)(2,1)S(1)}, bf16[64,2048]{1,0:T(8,128)(2,1)}, u32[]{:S(2)}) copy-start(bf16[64,2048]{1,0:T(8,128)(2,1)} %param.11) | copy-start | bytes 786436

commit v3 on v2

--- a/solution.py
+++ b/solution.py
@@ -454,6 +454,109 @@
     )(partial)
 
 
+def expert_kernel(plan, first_ref, rows_ref, gate_ref, up_ref, down_ref, out_ref, x_buf, weight_buf, sum_buf, result_buf):
+    groups, tok_rows, top, capacity, reps, chunks, width = plan
+    step = pl.program_id(0)
+    group_rows = rows_ref.shape[0]
+    seats = group_rows // tok_rows * capacity
+    slots = reps * seats
+
+    @pl.when(step < groups)
+    def _():
+        side = rows_ref[:, width:].astype(jnp.float32)
+        row = lax.broadcasted_iota(jnp.int32, (group_rows, 1), 0)
+        slot_iota = lax.broadcasted_iota(jnp.int32, (group_rows, slots), 1)
+        pick = jnp.zeros((group_rows, slots), jnp.float32)
+        upper, lower = pick, pick
+        for k in range(top):
+            replica = side[:, 2 * top + k : 2 * top + k + 1].astype(jnp.int32) - first_ref[0]
+            slot = side[:, 3 * top + k : 3 * top + k + 1].astype(jnp.int32)
+            here = (replica >= 0) & (replica < reps) & (slot < capacity)
+            seat = jnp.where(here, replica * seats + row // tok_rows * capacity + slot, -1)
+            hit = seat == slot_iota
+            pick = jnp.where(hit, 1.0, pick)
+            upper = jnp.where(hit, side[:, k : k + 1], upper)
+            lower = jnp.where(hit, side[:, top + k : top + k + 1], lower)
+        picked = jnp.dot(
+            pick.T.astype(jnp.bfloat16), rows_ref[:, :width], preferred_element_type=jnp.float32
+        ).astype(jnp.bfloat16)
+        for j in range(reps):
+            x_buf[j, pl.ds(step * seats, seats)] = picked[j * seats : (j + 1) * seats]
+        weight_buf[step, :, :slots] = upper.astype(jnp.bfloat16)
+        weight_buf[step, :, slots:] = lower.astype(jnp.bfloat16)
+
+    turn = step - groups
+
+    @pl.when((turn >= 0) & (turn < reps * chunks))
+    def _():
+        j, chunk = turn // chunks, turn % chunks
+        expert_in = x_buf[j]
+        gate = jnp.dot(expert_in, gate_ref[0], preferred_element_type=jnp.float32)
+        raised = jnp.dot(expert_in, up_ref[0], preferred_element_type=jnp.float32)
+        hidden = (gate / (1.0 + jnp.exp(-gate)) * raised).astype(jnp.bfloat16)
+        part = jnp.dot(hidden, down_ref[0], preferred_element_type=jnp.float32)
+
+        @pl.when(chunk == 0)
+        def _():
+            sum_buf[...] = part
+
+        @pl.when(chunk > 0)
+        def _():
+            sum_buf[...] += part
+
+        @pl.when(chunk == chunks - 1)
+        def _():
+            for g in range(groups):
+                result = sum_buf[g * seats : (g + 1) * seats].astype(jnp.bfloat16)
+                result_buf[g, pl.ds(j * seats, seats)] = result
+                result_buf[g, pl.ds(slots + j * seats, seats)] = result
+
+    group = turn - reps * chunks
+
+    @pl.when(group >= 0)
+    def _():
+        out_ref[...] = jnp.dot(
+            weight_buf[group], result_buf[group], preferred_element_type=jnp.float32
+        ).astype(out_ref.dtype)
+
+
+def run_experts(first, rows, up_gate, down, tok_rows, top, capacity):
+    row_total, padded = rows.shape
+    reps, hidden_units, width = down.shape
+    group_rows, chunks = 4 * tok_rows, 2
+    groups = row_total // group_rows
+    piece = hidden_units // chunks
+    seats = 4 * capacity
+    slots = reps * seats
+    turns = reps * chunks
+
+    def turn_of(step):
+        return jnp.clip(step - groups, 0, turns - 1)
+
+    return pl.pallas_call(
+        functools.partial(expert_kernel, (groups, tok_rows, top, capacity, reps, chunks, width)),
+        grid=(2 * groups + turns,),
+        out_shape=jax.ShapeDtypeStruct((row_total, width), jnp.bfloat16),
+        in_specs=[
+            pl.BlockSpec(memory_space=pltpu.SMEM),
+            pl.BlockSpec((group_rows, padded), lambda s: (jnp.minimum(s, groups - 1), 0)),
+            pl.BlockSpec((1, width, piece), lambda s: (turn_of(s) // chunks, 0, turn_of(s) % chunks)),
+            pl.BlockSpec((1, width, piece), lambda s: (turn_of(s) // chunks, 0, chunks + turn_of(s) % chunks)),
+            pl.BlockSpec((1, piece, width), lambda s: (turn_of(s) // chunks, turn_of(s) % chunks, 0)),
+        ],
+        out_specs=pl.BlockSpec((group_rows, width), lambda s: (jnp.maximum(s - groups - turns, 0), 0)),
+        scratch_shapes=[
+            pltpu.VMEM((reps, groups * seats, width), jnp.bfloat16),
+            pltpu.VMEM((groups, group_rows, 2 * slots), jnp.bfloat16),
+            pltpu.VMEM((groups * seats, width), jnp.float32),
+            pltpu.VMEM((groups, 2 * slots, width), jnp.bfloat16),
+        ],
+        compiler_params=pltpu.CompilerParams(
+            dimension_semantics=("arbitrary",), vmem_limit_bytes=52 << 20
+        ),
+    )(first, rows, up_gate, up_gate, down)
+
+
 SIDE = 128
 
 
@@ -474,11 +577,9 @@
     top_count = expert_ids.shape[1]
     replica_total = replica_expert.shape[0]
     local_reps = up_gate.shape[0]
-    hidden_units = down.shape[1]
     blocks = lax.axis_size("dp") * lax.axis_size("expert")
     me = lax.axis_index("dp") * lax.axis_size("expert") + lax.axis_index("expert")
     capacity = max(2, 2 * tok_rows * top_count // replica_total)
-    local_slots = local_reps * capacity
     side = jnp.pad(router, ((0, 0), (0, SIDE - expert_total)))
     proj_rows = gather_rows(jnp.concatenate([out_proj, side], axis=1), 0)
     proj_rows = proj_rows.reshape(blocks * out_proj.shape[0], model_width + SIDE)
@@ -500,35 +601,16 @@
     )
     side = jnp.pad(side, ((0, 0), (0, SIDE - 4 * top_count)))
     all_rows = gather_rows(jnp.concatenate([normed, side], axis=1), 1)
-    side = all_rows[:, :, model_width : model_width + 4 * top_count]
-    upper, lower, replica, slot_index = [
-        side[:, :, part * top_count : (part + 1) * top_count] for part in range(4)
-    ]
-    replica = replica.astype(jnp.int32) - me * local_reps
-    slot_index = slot_index.astype(jnp.int32)
-    place_here = jnp.where(slot_index < capacity, replica * capacity + slot_index, -1)
-    hits = place_here[:, :, :, None] == lax.iota(jnp.int32, local_slots)
-    pick = jnp.any(hits, axis=2).astype(jnp.bfloat16)
-    upper = jnp.sum(jnp.where(hits, upper[:, :, :, None], 0), axis=2)
-    lower = jnp.sum(jnp.where(hits, lower[:, :, :, None], 0), axis=2)
-    expert_in = jnp.einsum(
-        "btjc,btd->jbcd",
-        pick.reshape(blocks, tok_rows, local_reps, capacity),
-        all_rows,
-        preferred_element_type=jnp.float32,
-    ).astype(jnp.bfloat16)
-    expert_in = expert_in[..., :model_width].reshape(local_reps, blocks * capacity, model_width)
-    gate_up = jnp.einsum("jsd,jdf->jsf", expert_in, up_gate, preferred_element_type=jnp.float32)
-    hidden_act = (jax.nn.silu(gate_up[..., :hidden_units]) * gate_up[..., hidden_units:]).astype(
-        jnp.bfloat16
-    )
-    expert_out = jnp.einsum("jsf,jfd->jsd", hidden_act, down, preferred_element_type=jnp.float32)
-    expert_out = expert_out.astype(jnp.bfloat16).reshape(local_reps, blocks, capacity, model_width)
-    split = jnp.stack([upper, lower]).reshape(2, blocks, tok_rows, local_reps, capacity)
-    twice = jnp.broadcast_to(expert_out[None], (2,) + expert_out.shape)
-    partial = jnp.einsum(
-        "hbtjc,hjbcd->btd", split, twice, preferred_element_type=jnp.float32
-    ).astype(jnp.bfloat16)
+    first = jnp.full((1,), me * local_reps, jnp.int32)
+    partial = run_experts(
+        first,
+        all_rows.reshape(blocks * tok_rows, model_width + SIDE),
+        up_gate,
+        down,
+        tok_rows,
+        top_count,
+        capacity,
+    ).reshape(blocks, tok_rows, model_width)
     combined = scatter_sum(partial, 2)
     return (residual + combined.astype(jnp.float32)).astype(jnp.bfloat16)
 

time: 206 us -> 192 us (0.932)
  matrix products: 53.4 us -> 6.46 us
  Pallas kernels: 134 us -> 174 us
  other arithmetic: 13.4 us -> 9.37 us
  local copies, waits for them, and re-layouts: 4.19 us -> 1.9 us
    dot_general x3 -> x0, matrix products: 39.9 us -> none  [the longest x1 18.3 us: per_device_gathered(): jnp.einsum('jsd,jdf->jsf', expert_in, up_gate, preferred_element_type=jnp...]
    pallas_call x0 -> x1, Pallas kernels: none -> 39.7 us  [run_experts(): pl.pallas_call(functools.partial(expert_kernel, (groups, tok_rows, top, c...]
    unnamed x1 -> x0, matrix products: 7.06 us -> none
where the time goes in v3:
time: 192 us
  Pallas kernels  174 us (91%)
  other arithmetic  9.37 us (5%)
  matrix products  6.46 us (3%)
    pallas_call x2, Pallas kernels, gather_rows(): pl.pallas_call(functools.partial(gather_kernel, rows // 2), out_shape=jax...  89.8 us
    pallas_call x1, Pallas kernels, scatter_sum(): pl.pallas_call(functools.partial(scatter_kernel, half), out_shape=jax.Sha...  44.7 us
    pallas_call x1, Pallas kernels, run_experts(): pl.pallas_call(functools.partial(expert_kernel, (groups, tok_rows, top, c...  39.7 us
    dot_general x1, matrix products, per_device_gathered(): jnp.dot(context, proj_rows, preferred_element_type=jnp.float32)  5.19 us

profile of v3, /device:TPU:0, one launch (start us, length us, event | category | flops | bytes accessed | tf_op | source)
XLA Modules:
  0.0 192.0 jit_solution(5144368605618707552)
XLA Ops:
  0.0 0.0 copy-start
  0.0 0.9 convert_reduce_fusion.1
  0.9 0.8 copy.20
  1.7 1.9 fusion.5
  3.6 0.8 copy.24
  4.4 0.4 add_select_fusion
  4.7 2.0 %select_reduce_fusion = s32[64,8]{1,0:T(8,128)S(1)} fusion(s32[64,8]{1,0:T(8,128)S(1)} %add_select_fusion, s32[128]{0:T(128)S(1)} %convert_reduce_fusion.1, s32[128]{0:T(128)} %param.16, s32[64,8]{1,0:T(8,128)S(1)} %copy.20), kind=kLoop, calls=%fused_computation.17 | loop fusion | flops 327168 | bytes 7168 | tf_op jit(solution)/shard_map/reduce_sum | solution.py:26
  6.7 0.1 eq.84
  6.8 0.2 convert_reduce_fusion
  7.1 0.1 convert_element_type.53
  7.2 1.7 fusion.4.in_ref
  8.9 45.6 %shard_map.100 = bf16[32,64,2176]{2,1,0:T(8,128)(2,1)} custom-call(bf16[64,2176]{1,0:T(8,128)(2,1)} %fusion.4.in_ref), custom_call_target="tpu_custom_call" | custom-call | tf_op jit(solution)/shard_map/pallas_call | solution.py:265
  54.5 0.0 copy-start.2
  54.5 0.0 copy-start.3
  54.5 0.0 copy-done
  54.5 5.2 %convolution_bitcast_fusion = f32[64,2176]{1,0:T(8,128)S(1)} fusion(bf16[64,2048]{1,0:T(8,128)(2,1)S(1)} %copy-done, bf16[2048,2176]{1,0:T(8,128)(2,1)} %bitcast.9), kind=kOutput, calls=%fused_computation | convolution fusion | flops 570425344 | bytes 9732096 | tf_op jit(solution)/shard_map/dot_general | solution.py:589
  59.7 0.0 copy-done.2
  59.7 0.2 multiply_reduce_fusion
  59.9 0.0 copy-done.3
  59.9 0.1 multiply_convert_fusion
  60.0 1.3 fusion.2
  61.3 0.2 select_reduce_fusion.1
  61.5 0.1 copy.21
  61.6 0.1 copy.22
  61.7 0.1 fusion.14
  61.8 0.1 fusion.13
  61.9 0.7 pad_maximum_fusion.in_ref
  62.6 44.2 %shard_map.101 = bf16[32,64,2176]{2,1,0:T(8,128)(2,1)} custom-call(bf16[64,2176]{1,0:T(8,128)(2,1)} %pad_maximum_fusion.in_ref), custom_call_target="tpu_custom_call" | custom-call | tf_op jit(solution)/shard_map/pallas_call | solution.py:265
  106.8 0.0 copy-start.1
  106.8 39.7 %shard_map.102 = bf16[2048,2048]{1,0:T(8,128)(2,1)} custom-call(s32[1]{0:T(128)} %bitcast.2.first_ref, bf16[2048,2176]{1,0:T(8,128)(2,1)} %bitcast.11, bf16[4,2048,2048]{2,1,0:T(8,128)(2,1)} %up_ref.1, bf16[4,2048,2048]{2,1,0:T(8,128)(2,1)} %up_ref.1, bf16[4,1024,2048]{2,1,0:T(8,128)(2,1)} %down_ref.1), custom_call_target="tpu_custom_call" | custom-call | tf_op jit(solution)/shard_map/pallas_call | solution.py:536
  146.5 44.7 %shard_map.103 = bf16[64,2048]{1,0:T(8,128)(2,1)S(1)} custom-call(bf16[32,64,2048]{2,1,0:T(8,128)(2,1)} %bitcast.12), custom_call_target="tpu_custom_call" | custom-call | tf_op jit(solution)/shard_map/pallas_call | solution.py:430
  191.2 0.8 add_convert_fusion
  192.0 0.0 copy-done.1
  (4 shorter events, 0.0 us)
Async XLA Ops:
  0.0 54.5 %copy-start = (bf16[64,2048]{1,0:T(8,128)(2,1)S(1)}, bf16[64,2048]{1,0:T(8,128)(2,1)}, u32[]{:S(2)}) copy-start(bf16[64,2048]{1,0:T(8,128)(2,1)} %param.11) | copy-start | bytes 786436
  54.5 5.2 %copy-start.2 = (bf16[64,2048]{1,0:T(8,128)(2,1)S(1)}, bf16[64,2048]{1,0:T(8,128)(2,1)}, u32[]{:S(2)}) copy-start(bf16[64,2048]{1,0:T(8,128)(2,1)} %param.10) | copy-start | bytes 786436
  54.5 5.4 %copy-start.3 = (f32[2048]{0:T(1024)S(1)}, f32[2048]{0:T(1024)}, u32[]{:S(2)}) copy-start(f32[2048]{0:T(1024)} %param.13) | copy-start | bytes 24580
  106.8 85.1 %copy-start.1 = (bf16[64,2048]{1,0:T(8,128)(2,1)S(1)}, bf16[64,2048]{1,0:T(8,128)(2,1)}, u32[]{:S(2)}) copy-start(bf16[64,2048]{1,0:T(8,128)(2,1)} %param.11) | copy-start | bytes 786436
